TPU v7x, 32 devices: a whole 2x2x4 slice. The times are simulated.
32 devices in a mesh: rows: 4 (over y, x), cols: 8 (over z, core).
Axes of the slice: x: 2, y: 2, z: 4, core: 2. Of those that a mesh axis runs over, the one named last changes fastest.
Arguments:
- tokens: bfloat16 [128, 256, 256], P('rows', 'cols'), may hold values from -45 to 45
- key_bias: bfloat16 [128, 256], P('rows', 'cols'), may hold values from -3 to 250
- cotangent: bfloat16 [128, 256, 256], P('rows', 'cols'), may hold values from -6 to 6
- gain_row: float32 [256], replicated, may hold values from 0.1 to 1.9
- w_qkv_row: bfloat16 [256, 768], replicated, may hold values from -0.375 to 0.375
- w_out_row: bfloat16 [256, 256], replicated, may hold values from -0.375 to 0.375
- gain_col: float32 [256], replicated, may hold values from 0.1 to 1.9
- w_qkv_col: bfloat16 [256, 768], replicated, may hold values from -0.375 to 0.375
- w_out_col: bfloat16 [256, 256], replicated, may hold values from -0.375 to 0.375
- gain_mlp: float32 [256], replicated, may hold values from 0.1 to 1.9
- w_up: bfloat16 [256, 1024], replicated, may hold values from -0.375 to 0.375
- w_down: bfloat16 [1024, 256], replicated, may hold values from -0.1875 to 0.1875
Outputs:
- d_tokens: bfloat16 [128, 256, 256], P('rows', 'cols')
- d_gain_row: float32 [256], replicated
- d_w_qkv_row: float32 [256, 768], replicated
- d_w_out_row: float32 [256, 256], replicated
- d_gain_col: float32 [256], replicated
- d_w_qkv_col: float32 [256, 768], replicated
- d_w_out_col: float32 [256, 256], replicated
- d_gain_mlp: float32 [256], replicated
- d_w_up: float32 [256, 1024], replicated
- d_w_down: float32 [1024, 256], replicated
All inputs are finite; a program needn't handle non-finite values.
Results may differ from a plain program's by a relative error of at most 0.015.
Values may be sent and summed in bfloat16 or wider, within the bound.
No kernel may reach another device: no remote copies, remote signals or barrier semaphores. Data moves between devices by JAX's collectives and lax.ppermute only.
A program may use at most 128 MiB of HBM per device.

v0:
```python
import jax
import jax.numpy as jnp
from jax import lax
from jax.sharding import PartitionSpec as P

HEADS = 4


def product(spec_text, left_op, right_op):
    return jnp.einsum(spec_text, left_op, right_op, preferred_element_type=jnp.float32)


def layer_norm(entries, gain_vec):
    floats = entries.astype(jnp.float32)
    centred = floats - jnp.mean(floats, axis=-1, keepdims=True)
    inverse = lax.rsqrt(jnp.mean(centred * centred, axis=-1, keepdims=True) + 1e-05)
    normed = centred * inverse
    return ((normed * gain_vec).astype(jnp.bfloat16), normed, inverse)


def norm_back(grad_out, normed, inverse, gain_vec):
    scaled = grad_out * gain_vec
    result = inverse * (
        scaled
        - jnp.mean(scaled, axis=-1, keepdims=True)
        - normed * jnp.mean(scaled * normed, axis=-1, keepdims=True)
    )
    gain_grad = jnp.sum((grad_out * normed).reshape(-1, gain_vec.shape[0]), axis=0)
    return (result, gain_grad)


def over_cells(left_op, right_op):
    left_flat = left_op.reshape(-1, left_op.shape[-1])
    right_flat = right_op.reshape(-1, right_op.shape[-1])
    return lax.dot_general(
        left_flat, right_flat, (((0,), (0,)), ((), ())), preferred_element_type=jnp.float32
    )


def times_transpose(entries, weight):
    return lax.dot_general(
        entries, weight, (((entries.ndim - 1,), (1,)), ((), ())), preferred_element_type=jnp.float32
    )


def letters(length_axis):
    if length_axis == 1:
        return ("sqhd,skhd->shqk", "shqk,skhd->sqhd", "shqk,sqhd->skhd")
    return ("qshd,kshd->shqk", "shqk,kshd->qshd", "shqk,qshd->kshd")


def split_heads(packed, head_count):
    features = packed.shape[-1] // 3
    head_shape = packed.shape[:-1] + (head_count, features // head_count)
    return tuple(
        (
            packed[..., member * features : (member + 1) * features].reshape(head_shape)
            for member in range(3)
        )
    )


def key_terms(bias_rows, length_axis):
    floats = bias_rows.astype(jnp.float32)
    if length_axis == 0:
        floats = floats.T
    return floats[:, None, None, :]


def attention_weights(query_block, key_rows, bias_terms, factor, length_axis):
    scores = product(letters(length_axis)[0], query_block, key_rows) * factor + bias_terms
    shifted = jnp.exp(scores - jnp.max(scores, axis=-1, keepdims=True))
    return shifted / jnp.sum(shifted, axis=-1, keepdims=True)


def join_blocks(stacked, length_axis, features):
    if length_axis == 0:
        return stacked.reshape((-1, stacked.shape[2], features))
    reordered = jnp.moveaxis(stacked, 0, 1)
    return reordered.reshape((reordered.shape[0], -1, features))


def attend(packed, bias_rows, head_count, length_axis):
    query_rows, key_rows, value_rows = split_heads(packed, head_count)
    length = packed.shape[length_axis]
    block_len = min(length, 512)
    factor = query_rows.shape[-1] ** (-0.5)
    bias_terms = key_terms(bias_rows, length_axis)
    mixing = letters(length_axis)[1]

    def one_block(offset):
        query_block = lax.dynamic_slice_in_dim(query_rows, offset, block_len, length_axis)
        weights = attention_weights(query_block, key_rows, bias_terms, factor, length_axis)
        return product(mixing, weights.astype(jnp.bfloat16), value_rows).astype(jnp.bfloat16)

    offsets = jnp.arange(length // block_len, dtype=jnp.int32) * block_len
    return join_blocks(lax.map(one_block, offsets), length_axis, packed.shape[-1] // 3)


def attend_back(grad_out, packed, bias_rows, head_count, length_axis):
    query_rows, key_rows, value_rows = split_heads(packed, head_count)
    features = packed.shape[-1] // 3
    grad_heads = grad_out.reshape(query_rows.shape)
    length = packed.shape[length_axis]
    block_len = min(length, 512)
    factor = query_rows.shape[-1] ** (-0.5)
    bias_terms = key_terms(bias_rows, length_axis)
    score_spec, mixing, gather_spec = letters(length_axis)

    def one_block(running, offset):
        key_grad, value_grad = running
        query_block = lax.dynamic_slice_in_dim(query_rows, offset, block_len, length_axis)
        grad_block = lax.dynamic_slice_in_dim(grad_heads, offset, block_len, length_axis)
        weights = attention_weights(query_block, key_rows, bias_terms, factor, length_axis)
        weights_low = weights.astype(jnp.bfloat16)
        weight_grad = product(score_spec, grad_block, value_rows)
        centre = jnp.sum(weights * weight_grad, axis=-1, keepdims=True)
        score_grad = (weights * (weight_grad - centre) * factor).astype(jnp.bfloat16)
        query_grad = product(mixing, score_grad, key_rows)
        key_grad = key_grad + product(gather_spec, score_grad, query_block)
        value_grad = value_grad + product(gather_spec, weights_low, grad_block)
        return ((key_grad, value_grad), query_grad)

    empty_grad = jnp.zeros(key_rows.shape, jnp.float32)
    offsets = jnp.arange(length // block_len, dtype=jnp.int32) * block_len
    (key_grad, value_grad), query_parts = lax.scan(one_block, (empty_grad, empty_grad), offsets)
    query_grad = join_blocks(query_parts, length_axis, features)
    flat_shape = packed.shape[:-1] + (features,)
    joined = jnp.concatenate(
        [query_grad, key_grad.reshape(flat_shape), value_grad.reshape(flat_shape)], axis=-1
    )
    return joined.astype(jnp.bfloat16)


def attention_forward(inputs, bias_rows, gain_vec, w_qkv, w_out, head_count, length_axis):
    normal_in, normed, inverse = layer_norm(inputs, gain_vec)
    packed = jnp.dot(normal_in, w_qkv, preferred_element_type=jnp.float32).astype(jnp.bfloat16)
    mixed_out = attend(packed, bias_rows, head_count, length_axis)
    output = (
        inputs.astype(jnp.float32) + jnp.dot(mixed_out, w_out, preferred_element_type=jnp.float32)
    ).astype(jnp.bfloat16)
    return (output, (normal_in, normed, inverse, packed, mixed_out))


def attention_backward(
    grad_out, saved_parts, bias_rows, gain_vec, w_qkv, w_out, head_count, length_axis
):
    normal_in, normed, inverse, packed, mixed_out = saved_parts
    out_grad = over_cells(mixed_out, grad_out)
    mixed_grad = times_transpose(grad_out, w_out).astype(jnp.bfloat16)
    packed_grad = attend_back(mixed_grad, packed, bias_rows, head_count, length_axis)
    qkv_grad = over_cells(normal_in, packed_grad)
    input_grad, gain_grad = norm_back(
        times_transpose(packed_grad, w_qkv), normed, inverse, gain_vec
    )
    return (
        (grad_out.astype(jnp.float32) + input_grad).astype(jnp.bfloat16),
        (gain_grad, qkv_grad, out_grad),
    )


def feed_backward(inputs, grad_out, gain_vec, w_up, w_down):
    normal_in, normed, inverse = layer_norm(inputs, gain_vec)
    hidden = jnp.dot(normal_in, w_up, preferred_element_type=jnp.float32)
    active, gelu_back = jax.vjp(jax.nn.gelu, hidden)
    active_low = active.astype(jnp.bfloat16)
    down_grad = over_cells(active_low, grad_out)
    hidden_grad = gelu_back(times_transpose(grad_out, w_down))[0].astype(jnp.bfloat16)
    up_grad = over_cells(normal_in, hidden_grad)
    input_grad, gain_grad = norm_back(times_transpose(hidden_grad, w_up), normed, inverse, gain_vec)
    return (
        (grad_out.astype(jnp.float32) + input_grad).astype(jnp.bfloat16),
        (gain_grad, up_grad, down_grad),
    )


def shards(
    tokens,
    key_bias,
    cotangent,
    gain_row,
    w_qkv_row,
    w_out_row,
    gain_col,
    w_qkv_col,
    w_out_col,
    gain_mlp,
    w_up,
    w_down,
):
    row_cells, row_bias = (
        lax.all_to_all(tokens, "cols", split_axis=0, concat_axis=1, tiled=True),
        lax.all_to_all(key_bias, "cols", split_axis=0, concat_axis=1, tiled=True),
    )
    after_rows, row_saved = attention_forward(
        row_cells, row_bias, gain_row, w_qkv_row, w_out_row, HEADS, 1
    )
    column_cells = lax.all_to_all(
        lax.all_to_all(after_rows, "cols", split_axis=1, concat_axis=0, tiled=True),
        "rows",
        split_axis=1,
        concat_axis=0,
        tiled=True,
    )
    column_grads, column_bias = (
        lax.all_to_all(cotangent, "rows", split_axis=1, concat_axis=0, tiled=True),
        lax.all_to_all(key_bias, "rows", split_axis=1, concat_axis=0, tiled=True),
    )
    after_cols, column_saved = attention_forward(
        column_cells, column_bias, gain_col, w_qkv_col, w_out_col, HEADS, 0
    )
    mid_grad, feed_grads = feed_backward(after_cols, column_grads, gain_mlp, w_up, w_down)
    cell_grad, attn_grads = attention_backward(
        mid_grad, column_saved, column_bias, gain_col, w_qkv_col, w_out_col, HEADS, 0
    )
    factor = float(
        tokens.shape[0] * tokens.shape[1] * lax.axis_size("rows") * lax.axis_size("cols")
    ) ** (-0.5)
    other_sums = tuple((grad_term * factor for grad_term in attn_grads + feed_grads))
    grad_rows = lax.all_to_all(
        lax.all_to_all(cell_grad, "rows", split_axis=0, concat_axis=1, tiled=True),
        "cols",
        split_axis=0,
        concat_axis=1,
        tiled=True,
    )
    token_grad_rows, row_grads = attention_backward(
        grad_rows, row_saved, row_bias, gain_row, w_qkv_row, w_out_row, HEADS, 1
    )
    d_tokens = lax.all_to_all(token_grad_rows, "cols", split_axis=1, concat_axis=0, tiled=True)
    row_sums = tuple((grad_term * factor for grad_term in row_grads))
    summed = lax.psum(
        (
            row_sums[0],
            row_sums[1],
            row_sums[2],
            other_sums[0],
            other_sums[1],
            other_sums[2],
            other_sums[3],
            other_sums[4],
            other_sums[5],
        ),
        ("rows", "cols"),
    )
    row_sums = summed[:3]
    other_sums = summed[3:]
    return (
        d_tokens,
        row_sums[0],
        row_sums[1],
        row_sums[2],
        other_sums[0],
        other_sums[1],
        other_sums[2],
        other_sums[3],
        other_sums[4],
        other_sums[5],
    )


def solution(mesh):
    in_specs = (
        P("rows", "cols", None),
        P("rows", "cols"),
        P("rows", "cols", None),
        P(),
        P(),
        P(),
        P(),
        P(),
        P(),
        P(),
        P(),
        P(),
    )
    out_specs = (P("rows", "cols", None), P(), P(), P(), P(), P(), P(), P(), P(), P())
    return jax.shard_map(shards, mesh=mesh, in_specs=in_specs, out_specs=out_specs, check_vma=False)
```

profile of v0, /device:TPU:0, one launch (start us, length us, event | category | flops | bytes accessed | tf_op | source)
XLA Modules:
  0.0 385.8 jit_solution(3843586543527307721)
XLA Ops:
  7.2 12.1 %all_to_all.134 = bf16[8,4,32]{2,1,0:T(4,128)(2,1)S(1)} all-to-all(bf16[8,4,32]{2,1,0:T(4,128)(2,1)} %bitcast.263), channel_id=1, replica_groups=mesh['rows'=4,'cols'=8] {'cols'}, dimensions={0} | all-to-all | bytes 4096 | tf_op jit(solution)/shard_map/all_to_all | solution.py:193
  19.3 3.6 all-to-all-start.1
  24.4 13.7 %all-to-all-done.1 = bf16[32,32,256]{2,1,0:T(8,128)(2,1)S(1)} async-done(((bf16[32,32,256]{2,1,0:T(8,128)(2,1)}), bf16[32,32,256]{2,1,0:T(8,128)(2,1)S(1)}, u32[]{:S(2)}, u32[]{:S(2)}) %all-to-all-start.1) | async-done | bytes 524320 | tf_op jit(solution)/shard_map/all_to_all | solution.py:192
  38.2 3.7 all-to-all-start.5
  46.3 4.7 %fusion.124 = (f32[4,4,256]{2,1,0:T(4,128)S(1)}, f32[4,4,256,256]{2,3,1,0:T(8,128)}) fusion(f32[4,256]{1,0:T(4,128)S(1)} %reshape.252, bf16[4,256,4,64]{1,3,2,0:T(8,128)(2,1)S(1)} %bitcast.249, bf16[4,256,4,64]{1,3,2,0:T(8,128)(2,1)} %bitcast.247), kind=kOutput, calls=%fused_computation.165 | convolution fusion | flops 138412288 | bytes 5263360 | tf_op jit(solution)/shard_map/while/body/eval_jaxpr/sub | solution.py:72
  51.0 2.7 convolution_convert_fusion.7
  56.1 3.5 all-to-all-start.3
  60.7 14.2 %all-to-all-done.3 = bf16[4,256,256]{2,0,1:T(4,128)(2,1)S(1)} async-done(((bf16[4,256,256]{2,0,1:T(4,128)(2,1)}), bf16[4,256,256]{2,0,1:T(4,128)(2,1)S(1)}, u32[]{:S(2)}, u32[]{:S(2)}) %all-to-all-start.3) | async-done | bytes 524320 | tf_op jit(solution)/shard_map/all_to_all | solution.py:199
  74.8 4.2 %all-to-all-start = ((bf16[32,32,256]{2,0,1:T(8,128)(2,1)}), bf16[32,32,256]{2,0,1:T(8,128)(2,1)S(1)}, u32[]{:S(2)}, u32[]{:S(2)}) async-start(bf16[32,32,256]{2,0,1:T(8,128)(2,1)} %copy.364), calls=%async_computation | async-start | bytes 1048576 | tf_op jit(solution)/shard_map/all_to_all | solution.py:206
  80.2 6.6 %all-to-all-done = bf16[32,32,256]{2,0,1:T(8,128)(2,1)S(1)} async-done(((bf16[32,32,256]{2,0,1:T(8,128)(2,1)}), bf16[32,32,256]{2,0,1:T(8,128)(2,1)S(1)}, u32[]{:S(2)}, u32[]{:S(2)}) %all-to-all-start) | async-done | bytes 524320 | tf_op jit(solution)/shard_map/all_to_all | solution.py:206
  86.9 3.7 all-to-all-start.4
  91.5 5.8 %all-to-all-done.4 = bf16[32,32,256]{2,0,1:T(8,128)(2,1)S(1)} async-done(((bf16[32,32,256]{2,0,1:T(8,128)(2,1)}), bf16[32,32,256]{2,0,1:T(8,128)(2,1)S(1)}, u32[]{:S(2)}, u32[]{:S(2)}) %all-to-all-start.4) | async-done | bytes 524320 | tf_op jit(solution)/shard_map/all_to_all | solution.py:198
  107.9 3.7 fusion.125
  115.3 2.8 multiply_convert_fusion
  118.2 3.2 fusion.10
  127.3 3.5 convolution_convert_fusion.5
  132.6 5.2 %fusion.42 = bf16[8,4,64,128]{3,2,1,0:T(8,128)(2,1)} fusion(bf16[128,8,4,64]{0,3,2,1:T(8,128)(2,1)} %bitcast.252, f32[8,4,128,128]{2,3,1,0:T(8,128)} %fusion.126, f32[8,4,128,128]{2,3,1,0:T(8,128)} %get-tuple-element.127, f32[8,4,128]{2,1,0:T(4,128)S(1)} %get-tuple-element.126), kind=kOutput, calls=%fused_computation.49 | convolution fusion | flops 71045248 | bytes 5259264 | tf_op jit(solution)/shard_map/while/body/eval_jaxpr/shqk,kshd->qshd/dot_general | solution.py:10
  137.9 5.0 %fusion.45 = bf16[8,4,64,128]{3,2,1,0:T(8,128)(2,1)} fusion(bf16[128,8,4,64]{0,3,2,1:T(8,128)(2,1)S(1)} %bitcast.254, f32[8,4,128,128]{2,3,1,0:T(8,128)} %fusion.126, f32[8,4,128,128]{2,3,1,0:T(8,128)} %get-tuple-element.127, f32[8,4,128]{2,1,0:T(4,128)S(1)} %get-tuple-element.126), kind=kOutput, calls=%fused_computation.50 | convolution fusion | flops 71045248 | bytes 5259264 | tf_op jit(solution)/shard_map/while/body/eval_jaxpr/shqk,qshd->kshd/dot_general | solution.py:10
  148.4 3.2 multiply_reduce_fusion.2
  153.6 4.1 %all-to-all-start.6 = ((bf16[128,8,256]{2,1,0:T(8,128)(2,1)}), bf16[128,8,256]{2,1,0:T(8,128)(2,1)}, u32[]{:S(2)}, u32[]{:S(2)}) async-start(bf16[128,8,256]{2,1,0:T(8,128)(2,1)} %copy.399), calls=%async_computation.6 | async-start | bytes 1048576 | tf_op jit(solution)/shard_map/all_to_all | solution.py:221
  166.3 3.5 all-to-all-start.7
  172.3 3.0 fusion.56
  177.3 2.4 fusion.39
  179.7 5.3 %all-to-all-done.7 = bf16[32,32,256]{2,1,0:T(8,128)(2,1)S(1)} async-done(((bf16[32,32,256]{2,1,0:T(8,128)(2,1)}), bf16[32,32,256]{2,1,0:T(8,128)(2,1)S(1)}, u32[]{:S(2)}, u32[]{:S(2)}) %all-to-all-start.7) | async-done | bytes 524320 | tf_op jit(solution)/shard_map/all_to_all | solution.py:220
  185.4 3.8 convolution_convert_fusion.4
  189.3 2.7 fusion.127
  192.0 8.0 %fusion.48 = bf16[4,4,64,256]{3,2,1,0:T(8,128)(2,1)} fusion(bf16[4,256,4,64]{1,3,2,0:T(8,128)(2,1)S(1)} %bitcast.248, f32[4,4,256,256]{2,3,1,0:T(8,128)} %fusion.127, f32[4,4,256,256]{2,3,1,0:T(8,128)} %get-tuple-element.125, f32[4,4,256]{2,1,0:T(4,128)S(1)} %get-tuple-element.124), kind=kOutput, calls=%fused_computation.51 | convolution fusion | flops 141824256 | bytes 9453568 | tf_op jit(solution)/shard_map/while/body/eval_jaxpr/shqk,skhd->sqhd/dot_general | solution.py:10
  200.0 8.0 %fusion.51 = bf16[4,4,64,256]{3,2,1,0:T(8,128)(2,1)} fusion(bf16[4,256,4,64]{1,3,2,0:T(8,128)(2,1)S(1)} %bitcast.250, f32[4,4,256,256]{2,3,1,0:T(8,128)} %fusion.127, f32[4,4,256,256]{2,3,1,0:T(8,128)} %get-tuple-element.125, f32[4,4,256]{2,1,0:T(4,128)S(1)} %get-tuple-element.124), kind=kOutput, calls=%fused_computation.52 | convolution fusion | flops 141824256 | bytes 9453568 | tf_op jit(solution)/shard_map/while/body/eval_jaxpr/shqk,sqhd->skhd/dot_general | solution.py:10
  214.5 2.7 fusion.57
  221.9 3.5 all-to-all-start.8
  225.4 41.2 %all-reduce = (f32[256]{0:T(256)}, f32[256]{0:T(256)}, f32[256]{0:T(256)}) all-reduce(f32[256]{0:T(256)S(1)} %broadcast_multiply_fusion.11, f32[256]{0:T(256)S(1)} %broadcast_multiply_fusion.10, f32[256]{0:T(256)S(1)} %broadcast_multiply_fusion.9), channel_id=1, replica_groups=mesh['rows'=4,'cols'=8] {'rows','cols'}, use_global_device_ids=true, to_apply=%region_19.20 | all-reduce | flops 768 | bytes 6144 | tf_op jit(solution)/shard_map/psum | solution.py:232
  267.6 102.7 %all-reduce.4.cloned.1.call-done = (f32[256,768]{1,0:T(8,128)}, f32[256,256]{1,0:T(8,128)}, f32[256,768]{1,0:T(8,128)}, f32[256,256]{1,0:T(8,128)}, f32[256,1024]{1,0:T(8,128)}, /*index=5*/f32[1024,256]{1,0:T(8,128)}) async-done(((f32[256,768]{1,0:T(8,128)}, f32[256,256]{1,0:T(8,128)}, f32[256,768]{1,0:T(8,128)}, f32[256,256]{1,0:T(8,128)}, f32[256,1024]{1,0:T(8,128)}, /*index=5*/f32[1024,256]{1,0:T(8,128)}), ...) | async-done | bytes 4194320 | tf_op jit(solution)/shard_map/psum | solution.py:232
  (194 shorter events, 75.1 us)
Async XLA Ops:
  7.2 108.1 %copy-start = (bf16[256,1024]{1,0:T(8,128)(2,1)S(1)}, bf16[256,1024]{1,0:T(8,128)(2,1)}, u32[]{:S(2)}) copy-start(bf16[256,1024]{1,0:T(8,128)(2,1)} %param.22) | copy-start | bytes 1572868
  19.3 23.7 %copy-start.41 = (f32[256]{0:T(256)S(1)}, f32[256]{0:T(256)}, u32[]{:S(2)}) copy-start(f32[256]{0:T(256)} %param.15) | copy-start | bytes 3076
  19.3 18.9 %all-to-all-start.1 = ((bf16[32,32,256]{2,1,0:T(8,128)(2,1)}), bf16[32,32,256]{2,1,0:T(8,128)(2,1)S(1)}, u32[]{:S(2)}, u32[]{:S(2)}) async-start(bf16[32,32,256]{2,1,0:T(8,128)(2,1)} %param.12), calls=%async_computation.1 | async-start | bytes 1048576 | tf_op jit(solution)/shard_map/all_to_all | solution.py:192
  38.2 17.9 %all-to-all-start.5 = ((bf16[4,2,128]{2,1,0:T(2,128)(2,1)}), bf16[4,2,128]{2,1,0:T(2,128)(2,1)S(1)}, u32[]{:S(2)}, u32[]{:S(2)}) async-start(bf16[4,2,128]{2,1,0:T(2,128)(2,1)} %reshape.268), calls=%async_computation.5 | async-start | bytes 4096 | tf_op jit(solution)/shard_map/all_to_all | solution.py:207
  46.0 4.9 %copy-start.29 = (bf16[4,256,256]{1,2,0:T(8,128)(2,1)}, bf16[4,256,256]{1,2,0:T(8,128)(2,1)S(1)}, u32[]{:S(2)}) copy-start(bf16[4,256,256]{1,2,0:T(8,128)(2,1)S(1)} %copy.369) | copy-start | bytes 1572868
  46.2 4.7 %copy-start.8 = (bf16[4,256,256]{1,2,0:T(8,128)(2,1)}, bf16[4,256,256]{1,2,0:T(8,128)(2,1)S(1)}, u32[]{:S(2)}) copy-start(bf16[4,256,256]{1,2,0:T(8,128)(2,1)S(1)} %copy.368) | copy-start | bytes 1572868
  53.7 5.9 %copy-start.27 = (bf16[32,32,256]{2,1,0:T(8,128)(2,1)S(1)}, bf16[32,32,256]{2,1,0:T(8,128)(2,1)}, u32[]{:S(2)}) copy-start(bf16[32,32,256]{2,1,0:T(8,128)(2,1)} %param.14) | copy-start | bytes 1572868
  56.1 18.8 %all-to-all-start.3 = ((bf16[4,256,256]{2,0,1:T(4,128)(2,1)}), bf16[4,256,256]{2,0,1:T(4,128)(2,1)S(1)}, u32[]{:S(2)}, u32[]{:S(2)}) async-start(bf16[4,256,256]{2,0,1:T(4,128)(2,1)} %copy.374), calls=%async_computation.3 | async-start | bytes 1048576 | tf_op jit(solution)/shard_map/all_to_all | solution.py:199
  74.8 12.0 %all-to-all-start = ((bf16[32,32,256]{2,0,1:T(8,128)(2,1)}), bf16[32,32,256]{2,0,1:T(8,128)(2,1)S(1)}, u32[]{:S(2)}, u32[]{:S(2)}) async-start(bf16[32,32,256]{2,0,1:T(8,128)(2,1)} %copy.364), calls=%async_computation | async-start | bytes 1048576 | tf_op jit(solution)/shard_map/all_to_all | solution.py:206
  86.9 11.8 %copy-start.2 = (bf16[32,32,256]{2,0,1:T(8,128)(2,1)}, bf16[32,32,256]{2,0,1:T(8,128)(2,1)S(1)}, u32[]{:S(2)}) copy-start(bf16[32,32,256]{2,0,1:T(8,128)(2,1)S(1)} %all-to-all-done) | copy-start | bytes 1572868
  86.9 10.4 %all-to-all-start.4 = ((bf16[32,32,256]{2,0,1:T(8,128)(2,1)}), bf16[32,32,256]{2,0,1:T(8,128)(2,1)S(1)}, u32[]{:S(2)}, u32[]{:S(2)}) async-start(bf16[32,32,256]{2,0,1:T(8,128)(2,1)} %copy.377), calls=%async_computation.4 | async-start | bytes 1048576 | tf_op jit(solution)/shard_map/all_to_all | solution.py:198
  90.7 8.9 %copy-start.40 = (f32[256]{0:T(256)S(1)}, f32[256]{0:T(256)}, u32[]{:S(2)}) copy-start(f32[256]{0:T(256)} %param.18) | copy-start | bytes 3076
  107.9 5.8 %copy-start.20 = (bf16[128,8,256]{0,2,1:T(8,128)(2,1)}, bf16[128,8,256]{0,2,1:T(8,128)(2,1)S(1)}, u32[]{:S(2)}) copy-start(bf16[128,8,256]{0,2,1:T(8,128)(2,1)S(1)} %copy.385) | copy-start | bytes 1572868
  132.6 5.2 %copy-start.32 = (bf16[128,8,256]{0,2,1:T(8,128)(2,1)S(1)}, bf16[128,8,256]{0,2,1:T(8,128)(2,1)}, u32[]{:S(2)}) copy-start(bf16[128,8,256]{0,2,1:T(8,128)(2,1)} %copy.386) | copy-start | bytes 1572868
  144.1 4.3 %copy-start.31 = (bf16[128,8,256]{2,0,1:T(8,128)(2,1)}, bf16[128,8,256]{2,0,1:T(8,128)(2,1)S(1)}, u32[]{:S(2)}) copy-start(bf16[128,8,256]{2,0,1:T(8,128)(2,1)S(1)} %copy.398) | copy-start | bytes 1572868
  151.6 6.1 %copy-start.3 = (bf16[32,32,256]{2,0,1:T(8,128)(2,1)S(1)}, bf16[32,32,256]{2,0,1:T(8,128)(2,1)}, u32[]{:S(2)}) copy-start(bf16[32,32,256]{2,0,1:T(8,128)(2,1)} %copy-done.2) | copy-start | bytes 1572868
  152.5 6.3 %copy-start.11 = (bf16[4,4,64,256]{3,2,1,0:T(8,128)(2,1)S(1)}, bf16[4,4,64,256]{3,2,1,0:T(8,128)(2,1)}, u32[]{:S(2)}) copy-start(bf16[4,4,64,256]{3,2,1,0:T(8,128)(2,1)} %copy-done.10) | copy-start | bytes 1572868
  153.6 10.8 %all-to-all-start.6 = ((bf16[128,8,256]{2,1,0:T(8,128)(2,1)}), bf16[128,8,256]{2,1,0:T(8,128)(2,1)}, u32[]{:S(2)}, u32[]{:S(2)}) async-start(bf16[128,8,256]{2,1,0:T(8,128)(2,1)} %copy.399), calls=%async_computation.6 | async-start | bytes 1048576 | tf_op jit(solution)/shard_map/all_to_all | solution.py:221
  159.2 10.9 %copy-start.6 = (bf16[128,8,256]{2,0,1:T(8,128)(2,1)S(1)}, bf16[128,8,256]{2,0,1:T(8,128)(2,1)}, u32[]{:S(2)}) copy-start(bf16[128,8,256]{2,0,1:T(8,128)(2,1)} %copy-done.4) | copy-start | bytes 1572868
  163.5 8.9 %copy-start.18 = (bf16[128,8,256]{2,0,1:T(8,128)(2,1)S(1)}, bf16[128,8,256]{2,0,1:T(8,128)(2,1)}, u32[]{:S(2)}) copy-start(bf16[128,8,256]{2,0,1:T(8,128)(2,1)} %copy-done.17) | copy-start | bytes 1572868
  166.3 18.8 %all-to-all-start.7 = ((bf16[32,32,256]{2,1,0:T(8,128)(2,1)}), bf16[32,32,256]{2,1,0:T(8,128)(2,1)S(1)}, u32[]{:S(2)}, u32[]{:S(2)}) async-start(bf16[32,32,256]{2,1,0:T(8,128)(2,1)} %bitcast.239), calls=%async_computation.7 | async-start | bytes 1048576 | tf_op jit(solution)/shard_map/all_to_all | solution.py:220
  169.8 200.5 %all-reduce.4.cloned.1.call-start = ((), (), s32[]{:S(2)}) async-start(), calls=%async_computation.9 | async-start | bytes 8388608 | tf_op jit(solution)/shard_map/psum | solution.py:232
  192.0 8.0 %copy-start.30 = (bf16[4,256,256]{1,2,0:T(8,128)(2,1)S(1)}, bf16[4,256,256]{1,2,0:T(8,128)(2,1)}, u32[]{:S(2)}) copy-start(bf16[4,256,256]{1,2,0:T(8,128)(2,1)} %copy-done.29) | copy-start | bytes 1572868
  208.0 5.5 %copy-start.19 = (bf16[32,8,4,256]{3,1,2,0:T(8,128)(2,1)S(1)}, bf16[32,8,4,256]{3,1,2,0:T(8,128)(2,1)}, u32[]{:S(2)}) copy-start(bf16[32,8,4,256]{3,1,2,0:T(8,128)(2,1)} %copy.437) | copy-start | bytes 1572868
  208.0 6.5 %copy-start.16 = (bf16[4,256,256]{2,1,0:T(8,128)(2,1)S(1)}, bf16[4,256,256]{2,1,0:T(8,128)(2,1)}, u32[]{:S(2)}) copy-start(bf16[4,256,256]{2,1,0:T(8,128)(2,1)} %copy-done.15) | copy-start | bytes 1572868
  219.8 5.6 %copy-start.42 = (f32[256]{0:T(256)S(1)}, f32[256]{0:T(256)}, u32[]{:S(2)}) copy-start(f32[256]{0:T(256)} %get-tuple-element.73) | copy-start | bytes 3076
  219.8 5.6 %copy-start.43 = (f32[256]{0:T(256)S(1)}, f32[256]{0:T(256)}, u32[]{:S(2)}) copy-start(f32[256]{0:T(256)} %get-tuple-element.84) | copy-start | bytes 3076
  221.9 44.8 %all-to-all-start.8 = ((bf16[4,256,256]{2,0,1:T(4,128)(2,1)}), bf16[4,256,256]{2,0,1:T(4,128)(2,1)S(1)}, u32[]{:S(2)}, u32[]{:S(2)}) async-start(bf16[4,256,256]{2,0,1:T(4,128)(2,1)} %copy.409), calls=%async_computation.8 | async-start | bytes 1048576 | tf_op jit(solution)/shard_map/all_to_all | solution.py:230
  370.2 6.0 %copy-start.38 = (f32[256,256]{1,0:T(8,128)S(1)}, f32[256,256]{1,0:T(8,128)}, u32[]{:S(2)}) copy-start(f32[256,256]{1,0:T(8,128)} %get-tuple-element.143) | copy-start | bytes 786436
  370.2 6.7 %copy-start.24 = (f32[256,1024]{1,0:T(8,128)S(1)}, f32[256,1024]{1,0:T(8,128)}, u32[]{:S(2)}) copy-start(f32[256,1024]{1,0:T(8,128)} %get-tuple-element.145) | copy-start | bytes 3145732
  370.2 7.7 %copy-start.23 = (f32[1024,256]{1,0:T(8,128)S(1)}, f32[1024,256]{1,0:T(8,128)}, u32[]{:S(2)}) copy-start(f32[1024,256]{1,0:T(8,128)} %get-tuple-element.146) | copy-start | bytes 3145732
  372.5 6.4 %copy-start.1 = (bf16[256,1024]{1,0:T(8,128)(2,1)S(1)}, bf16[256,1024]{1,0:T(8,128)(2,1)}, u32[]{:S(2)}) copy-start(bf16[256,1024]{1,0:T(8,128)(2,1)} %param.22) | copy-start | bytes 1572868
  (23 other events, 51.3 us)
Sparse Core Ops, SparseCore 0:
  217.3 152.8 all-reduce.3
where the time goes:
time: 387 us; the launch traced here: 386 us
  waiting for transfers between devices  149 us (39%)
  matrix products  80.4 us (21%)
  blocking collectives  53.3 us (14%)
  local copies, waits for them, and re-layouts  52.3 us (14%)
  starting transfers between devices  30.1 us (8%)
  between operations  14.7 us (4%)
  other arithmetic  5.81 us (2%)
    psum x1, waiting for transfers between devices, shards(): lax.psum((row_sums[0], row_sums[1], row_sums[2], other_sums[0], other_sum...  103 us
    dot_general x10, matrix products, product(): jnp.einsum(spec_text, left_op, right_op, preferred_element_type=jnp.float32)  42.8 us
    psum x1, blocking collectives, shards(): lax.psum((row_sums[0], row_sums[1], row_sums[2], other_sums[0], other_sum...  41.2 us
    unnamed x104, local copies, waits for them, and re-layouts  17.6 us
    all_to_all x1, waiting for transfers between devices, shards(): lax.all_to_all(after_rows, 'cols', split_axis=1, concat_axis=0, tiled=True)  14.2 us
    all_to_all x1, waiting for transfers between devices, shards(): lax.all_to_all(tokens, 'cols', split_axis=0, concat_axis=1, tiled=True)  13.7 us
    dot_general x6, matrix products, over_cells(): lax.dot_general(left_flat, right_flat, (((0,), (0,)), ((), ())), preferre...  13.3 us
    all_to_all x1, blocking collectives, shards(): lax.all_to_all(key_bias, 'cols', split_axis=0, concat_axis=1, tiled=True)  12.1 us
  transfers between devices with their start and end apart: 9, of which 7 were waited for; matrix products, arithmetic and copies ran while one was open for 10% of the time, Pallas kernels for 0%

commit v1 on v0

--- a/solution.py
+++ b/solution.py
@@ -190,7 +190,12 @@
 ):
     row_cells, row_bias = (
         lax.all_to_all(tokens, "cols", split_axis=0, concat_axis=1, tiled=True),
-        lax.all_to_all(key_bias, "cols", split_axis=0, concat_axis=1, tiled=True),
+        jnp.concatenate(
+            lax.all_to_all(
+                jnp.stack(jnp.split(key_bias, lax.axis_size("cols"), axis=0)), "cols", 0, 0
+            ),
+            axis=1,
+        ),
     )
     after_rows, row_saved = attention_forward(
         row_cells, row_bias, gain_row, w_qkv_row, w_out_row, HEADS, 1

time: 387 us -> 393 us (1.016)
  local copies, waits for them, and re-layouts: 52.3 us -> 58.2 us
    unnamed x104 -> x111, local copies, waits for them, and re-layouts: 17.6 us -> 21.7 us
  transfers between devices with their start and end apart: 9 -> 9, of which waited for: 7 -> 7; matrix products, arithmetic and copies ran while one was open for 10% -> 9% of each run, Pallas kernels for 0% -> 0%
where the time goes in v1:
time: 393 us; the launch traced here: 391 us
  waiting for transfers between devices  149 us (38%)
  matrix products  80.6 us (21%)
  local copies, waits for them, and re-layouts  58.2 us (15%)
  blocking collectives  53 us (13%)
  starting transfers between devices  30.1 us (8%)
  between operations  14.7 us (4%)
  other arithmetic  5.81 us (1%)
    psum x1, waiting for transfers between devices, shards(): lax.psum((row_sums[0], row_sums[1], row_sums[2], other_sums[0], other_sum...  103 us
    dot_general x10, matrix products, product(): jnp.einsum(spec_text, left_op, right_op, preferred_element_type=jnp.float32)  42.9 us
    psum x1, blocking collectives, shards(): lax.psum((row_sums[0], row_sums[1], row_sums[2], other_sums[0], other_sum...  41.3 us
    unnamed x111, local copies, waits for them, and re-layouts  21.7 us
    all_to_all x1, waiting for transfers between devices, shards(): lax.all_to_all(after_rows, 'cols', split_axis=1, concat_axis=0, tiled=True)  14.2 us
    all_to_all x1, waiting for transfers between devices, shards(): lax.all_to_all(tokens, 'cols', split_axis=0, concat_axis=1, tiled=True)  13.7 us
    dot_general x6, matrix products, over_cells(): lax.dot_general(left_flat, right_flat, (((0,), (0,)), ((), ())), preferre...  13.3 us
    all_to_all x1, blocking collectives, shards(): lax.all_to_all(jnp.stack(jnp.split(key_bias, lax.axis_size('cols'), axis=...  11.7 us
  transfers between devices with their start and end apart: 9, of which 7 were waited for; matrix products, arithmetic and copies ran while one was open for 9% of the time, Pallas kernels for 0%

profile of v1, /device:TPU:0, one launch (start us, length us, event | category | flops | bytes accessed | tf_op | source)
XLA Modules:
  0.0 391.4 jit_solution(10200569974729738327)
XLA Ops:
  12.8 11.7 %all_to_all.126 = bf16[8,4,32]{2,1,0:T(4,128)(2,1)S(1)} all-to-all(bf16[8,4,32]{2,1,0:T(4,128)(2,1)S(1)} %constant_dynamic-update-slice_fusion), channel_id=1, replica_groups=mesh['rows'=4,'cols'=8] {'cols'}, dimensions={0} | all-to-all | bytes 4096 | tf_op jit(solution)/shard_map/all_to_all | solution.py:194
  24.5 3.6 all-to-all-start.1
  29.7 13.7 %all-to-all-done.1 = bf16[32,32,256]{2,1,0:T(8,128)(2,1)S(1)} async-done(((bf16[32,32,256]{2,1,0:T(8,128)(2,1)}), bf16[32,32,256]{2,1,0:T(8,128)(2,1)S(1)}, u32[]{:S(2)}, u32[]{:S(2)}) %all-to-all-start.1) | async-done | bytes 524320 | tf_op jit(solution)/shard_map/all_to_all | solution.py:192
  43.4 3.7 all-to-all-start.5
  51.5 4.7 %fusion.124 = (f32[4,4,256]{2,1,0:T(4,128)S(1)}, f32[4,4,256,256]{2,3,1,0:T(8,128)}) fusion(f32[4,256]{1,0:T(4,128)S(1)} %reshape.251, bf16[4,256,4,64]{1,3,2,0:T(8,128)(2,1)S(1)} %bitcast.264, bf16[4,256,4,64]{1,3,2,0:T(8,128)(2,1)} %bitcast.262), kind=kOutput, calls=%fused_computation.173 | convolution fusion | flops 138412288 | bytes 5263360 | tf_op jit(solution)/shard_map/while/body/eval_jaxpr/sub | solution.py:72
  56.2 2.7 convolution_convert_fusion.7
  61.3 3.5 all-to-all-start.3
  65.9 14.2 %all-to-all-done.3 = bf16[4,256,256]{2,0,1:T(4,128)(2,1)S(1)} async-done(((bf16[4,256,256]{2,0,1:T(4,128)(2,1)}), bf16[4,256,256]{2,0,1:T(4,128)(2,1)S(1)}, u32[]{:S(2)}, u32[]{:S(2)}) %all-to-all-start.3) | async-done | bytes 524320 | tf_op jit(solution)/shard_map/all_to_all | solution.py:204
  80.1 4.2 %all-to-all-start = ((bf16[32,32,256]{2,0,1:T(8,128)(2,1)}), bf16[32,32,256]{2,0,1:T(8,128)(2,1)S(1)}, u32[]{:S(2)}, u32[]{:S(2)}) async-start(bf16[32,32,256]{2,0,1:T(8,128)(2,1)} %copy.363), calls=%async_computation | async-start | bytes 1048576 | tf_op jit(solution)/shard_map/all_to_all | solution.py:211
  85.5 6.6 %all-to-all-done = bf16[32,32,256]{2,0,1:T(8,128)(2,1)S(1)} async-done(((bf16[32,32,256]{2,0,1:T(8,128)(2,1)}), bf16[32,32,256]{2,0,1:T(8,128)(2,1)S(1)}, u32[]{:S(2)}, u32[]{:S(2)}) %all-to-all-start) | async-done | bytes 524320 | tf_op jit(solution)/shard_map/all_to_all | solution.py:211
  92.1 3.7 all-to-all-start.4
  96.8 5.7 %all-to-all-done.4 = bf16[32,32,256]{2,0,1:T(8,128)(2,1)S(1)} async-done(((bf16[32,32,256]{2,0,1:T(8,128)(2,1)}), bf16[32,32,256]{2,0,1:T(8,128)(2,1)S(1)}, u32[]{:S(2)}, u32[]{:S(2)}) %all-to-all-start.4) | async-done | bytes 524320 | tf_op jit(solution)/shard_map/all_to_all | solution.py:203
  113.6 3.7 fusion.125
  121.0 2.8 multiply_convert_fusion
  123.9 3.2 fusion.10
  133.0 3.5 convolution_convert_fusion.5
  138.3 5.2 %fusion.42 = bf16[8,4,64,128]{3,2,1,0:T(8,128)(2,1)} fusion(bf16[128,8,4,64]{0,3,2,1:T(8,128)(2,1)} %bitcast.267, f32[8,4,128,128]{2,3,1,0:T(8,128)} %fusion.126, f32[8,4,128,128]{2,3,1,0:T(8,128)} %get-tuple-element.127, f32[8,4,128]{2,1,0:T(4,128)S(1)} %get-tuple-element.126), kind=kOutput, calls=%fused_computation.49 | convolution fusion | flops 71045248 | bytes 5259264 | tf_op jit(solution)/shard_map/while/body/eval_jaxpr/shqk,kshd->qshd/dot_general | solution.py:10
  143.6 5.0 %fusion.45 = bf16[8,4,64,128]{3,2,1,0:T(8,128)(2,1)} fusion(bf16[128,8,4,64]{0,3,2,1:T(8,128)(2,1)S(1)} %bitcast.269, f32[8,4,128,128]{2,3,1,0:T(8,128)} %fusion.126, f32[8,4,128,128]{2,3,1,0:T(8,128)} %get-tuple-element.127, f32[8,4,128]{2,1,0:T(4,128)S(1)} %get-tuple-element.126), kind=kOutput, calls=%fused_computation.50 | convolution fusion | flops 71045248 | bytes 5259264 | tf_op jit(solution)/shard_map/while/body/eval_jaxpr/shqk,qshd->kshd/dot_general | solution.py:10
  154.1 3.2 multiply_reduce_fusion.2
  159.2 4.1 %all-to-all-start.6 = ((bf16[128,8,256]{2,1,0:T(8,128)(2,1)}), bf16[128,8,256]{2,1,0:T(8,128)(2,1)}, u32[]{:S(2)}, u32[]{:S(2)}) async-start(bf16[128,8,256]{2,1,0:T(8,128)(2,1)} %copy.398), calls=%async_computation.6 | async-start | bytes 1048576 | tf_op jit(solution)/shard_map/all_to_all | solution.py:226
  172.0 3.5 all-to-all-start.7
  178.0 3.0 fusion.56
  183.0 2.4 fusion.39
  185.4 5.3 %all-to-all-done.7 = bf16[32,32,256]{2,1,0:T(8,128)(2,1)S(1)} async-done(((bf16[32,32,256]{2,1,0:T(8,128)(2,1)}), bf16[32,32,256]{2,1,0:T(8,128)(2,1)S(1)}, u32[]{:S(2)}, u32[]{:S(2)}) %all-to-all-start.7) | async-done | bytes 524320 | tf_op jit(solution)/shard_map/all_to_all | solution.py:225
  191.1 3.8 convolution_convert_fusion.4
  195.0 2.7 fusion.127
  197.7 8.0 %fusion.48 = bf16[4,4,64,256]{3,2,1,0:T(8,128)(2,1)} fusion(bf16[4,256,4,64]{1,3,2,0:T(8,128)(2,1)S(1)} %bitcast.263, f32[4,4,256,256]{2,3,1,0:T(8,128)} %fusion.127, f32[4,4,256,256]{2,3,1,0:T(8,128)} %get-tuple-element.125, f32[4,4,256]{2,1,0:T(4,128)S(1)} %get-tuple-element.124), kind=kOutput, calls=%fused_computation.51 | convolution fusion | flops 141824256 | bytes 9453568 | tf_op jit(solution)/shard_map/while/body/eval_jaxpr/shqk,skhd->sqhd/dot_general | solution.py:10
  205.7 8.0 %fusion.51 = bf16[4,4,64,256]{3,2,1,0:T(8,128)(2,1)} fusion(bf16[4,256,4,64]{1,3,2,0:T(8,128)(2,1)S(1)} %bitcast.265, f32[4,4,256,256]{2,3,1,0:T(8,128)} %fusion.127, f32[4,4,256,256]{2,3,1,0:T(8,128)} %get-tuple-element.125, f32[4,4,256]{2,1,0:T(4,128)S(1)} %get-tuple-element.124), kind=kOutput, calls=%fused_computation.52 | convolution fusion | flops 141824256 | bytes 9453568 | tf_op jit(solution)/shard_map/while/body/eval_jaxpr/shqk,sqhd->skhd/dot_general | solution.py:10
  220.2 2.7 fusion.57
  227.6 3.5 all-to-all-start.8
  231.1 41.3 %all-reduce = (f32[256]{0:T(256)}, f32[256]{0:T(256)}, f32[256]{0:T(256)}) all-reduce(f32[256]{0:T(256)S(1)} %broadcast_multiply_fusion.11, f32[256]{0:T(256)S(1)} %broadcast_multiply_fusion.10, f32[256]{0:T(256)S(1)} %broadcast_multiply_fusion.9), channel_id=1, replica_groups=mesh['rows'=4,'cols'=8] {'rows','cols'}, use_global_device_ids=true, to_apply=%region_19.20 | all-reduce | flops 768 | bytes 6144 | tf_op jit(solution)/shard_map/psum | solution.py:237
  273.3 102.6 %all-reduce.4.cloned.1.call-done = (f32[256,768]{1,0:T(8,128)}, f32[256,256]{1,0:T(8,128)}, f32[256,768]{1,0:T(8,128)}, f32[256,256]{1,0:T(8,128)}, f32[256,1024]{1,0:T(8,128)}, /*index=5*/f32[1024,256]{1,0:T(8,128)}) async-done(((f32[256,768]{1,0:T(8,128)}, f32[256,256]{1,0:T(8,128)}, f32[256,768]{1,0:T(8,128)}, f32[256,256]{1,0:T(8,128)}, f32[256,1024]{1,0:T(8,128)}, /*index=5*/f32[1024,256]{1,0:T(8,128)}), ...) | async-done | bytes 4194320 | tf_op jit(solution)/shard_map/psum | solution.py:237
  (202 shorter events, 81.1 us)
Async XLA Ops:
  7.2 113.8 %copy-start = (bf16[256,1024]{1,0:T(8,128)(2,1)S(1)}, bf16[256,1024]{1,0:T(8,128)(2,1)}, u32[]{:S(2)}) copy-start(bf16[256,1024]{1,0:T(8,128)(2,1)} %param.22) | copy-start | bytes 1572868
  24.5 23.7 %copy-start.41 = (f32[256]{0:T(256)S(1)}, f32[256]{0:T(256)}, u32[]{:S(2)}) copy-start(f32[256]{0:T(256)} %param.15) | copy-start | bytes 3076
  24.5 18.9 %all-to-all-start.1 = ((bf16[32,32,256]{2,1,0:T(8,128)(2,1)}), bf16[32,32,256]{2,1,0:T(8,128)(2,1)S(1)}, u32[]{:S(2)}, u32[]{:S(2)}) async-start(bf16[32,32,256]{2,1,0:T(8,128)(2,1)} %param.12), calls=%async_computation.1 | async-start | bytes 1048576 | tf_op jit(solution)/shard_map/all_to_all | solution.py:192
  43.4 17.9 %all-to-all-start.5 = ((bf16[4,2,128]{2,1,0:T(2,128)(2,1)}), bf16[4,2,128]{2,1,0:T(2,128)(2,1)S(1)}, u32[]{:S(2)}, u32[]{:S(2)}) async-start(bf16[4,2,128]{2,1,0:T(2,128)(2,1)} %reshape.267), calls=%async_computation.5 | async-start | bytes 4096 | tf_op jit(solution)/shard_map/all_to_all | solution.py:212
  51.3 4.9 %copy-start.29 = (bf16[4,256,256]{1,2,0:T(8,128)(2,1)}, bf16[4,256,256]{1,2,0:T(8,128)(2,1)S(1)}, u32[]{:S(2)}) copy-start(bf16[4,256,256]{1,2,0:T(8,128)(2,1)S(1)} %copy.368) | copy-start | bytes 1572868
  51.5 4.7 %copy-start.8 = (bf16[4,256,256]{1,2,0:T(8,128)(2,1)}, bf16[4,256,256]{1,2,0:T(8,128)(2,1)S(1)}, u32[]{:S(2)}) copy-start(bf16[4,256,256]{1,2,0:T(8,128)(2,1)S(1)} %copy.367) | copy-start | bytes 1572868
  58.9 5.9 %copy-start.27 = (bf16[32,32,256]{2,1,0:T(8,128)(2,1)S(1)}, bf16[32,32,256]{2,1,0:T(8,128)(2,1)}, u32[]{:S(2)}) copy-start(bf16[32,32,256]{2,1,0:T(8,128)(2,1)} %param.14) | copy-start | bytes 1572868
  61.3 18.8 %all-to-all-start.3 = ((bf16[4,256,256]{2,0,1:T(4,128)(2,1)}), bf16[4,256,256]{2,0,1:T(4,128)(2,1)S(1)}, u32[]{:S(2)}, u32[]{:S(2)}) async-start(bf16[4,256,256]{2,0,1:T(4,128)(2,1)} %copy.373), calls=%async_computation.3 | async-start | bytes 1048576 | tf_op jit(solution)/shard_map/all_to_all | solution.py:204
  80.1 12.0 %all-to-all-start = ((bf16[32,32,256]{2,0,1:T(8,128)(2,1)}), bf16[32,32,256]{2,0,1:T(8,128)(2,1)S(1)}, u32[]{:S(2)}, u32[]{:S(2)}) async-start(bf16[32,32,256]{2,0,1:T(8,128)(2,1)} %copy.363), calls=%async_computation | async-start | bytes 1048576 | tf_op jit(solution)/shard_map/all_to_all | solution.py:211
  92.1 11.8 %copy-start.2 = (bf16[32,32,256]{2,0,1:T(8,128)(2,1)}, bf16[32,32,256]{2,0,1:T(8,128)(2,1)S(1)}, u32[]{:S(2)}) copy-start(bf16[32,32,256]{2,0,1:T(8,128)(2,1)S(1)} %all-to-all-done) | copy-start | bytes 1572868
  92.1 10.4 %all-to-all-start.4 = ((bf16[32,32,256]{2,0,1:T(8,128)(2,1)}), bf16[32,32,256]{2,0,1:T(8,128)(2,1)S(1)}, u32[]{:S(2)}, u32[]{:S(2)}) async-start(bf16[32,32,256]{2,0,1:T(8,128)(2,1)} %copy.376), calls=%async_computation.4 | async-start | bytes 1048576 | tf_op jit(solution)/shard_map/all_to_all | solution.py:203
  95.9 8.9 %copy-start.40 = (f32[256]{0:T(256)S(1)}, f32[256]{0:T(256)}, u32[]{:S(2)}) copy-start(f32[256]{0:T(256)} %param.18) | copy-start | bytes 3076
  105.2 5.0 %copy-start.17 = (bf16[128,8,256]{2,0,1:T(8,128)(2,1)}, bf16[128,8,256]{2,0,1:T(8,128)(2,1)S(1)}, u32[]{:S(2)}) copy-start(bf16[128,8,256]{2,0,1:T(8,128)(2,1)S(1)} %multiply_convert_fusion.3) | copy-start | bytes 1572868
  113.6 5.8 %copy-start.20 = (bf16[128,8,256]{0,2,1:T(8,128)(2,1)}, bf16[128,8,256]{0,2,1:T(8,128)(2,1)S(1)}, u32[]{:S(2)}) copy-start(bf16[128,8,256]{0,2,1:T(8,128)(2,1)S(1)} %copy.384) | copy-start | bytes 1572868
  138.3 5.2 %copy-start.32 = (bf16[128,8,256]{0,2,1:T(8,128)(2,1)S(1)}, bf16[128,8,256]{0,2,1:T(8,128)(2,1)}, u32[]{:S(2)}) copy-start(bf16[128,8,256]{0,2,1:T(8,128)(2,1)} %copy.385) | copy-start | bytes 1572868
  157.3 6.1 %copy-start.3 = (bf16[32,32,256]{2,0,1:T(8,128)(2,1)S(1)}, bf16[32,32,256]{2,0,1:T(8,128)(2,1)}, u32[]{:S(2)}) copy-start(bf16[32,32,256]{2,0,1:T(8,128)(2,1)} %copy-done.2) | copy-start | bytes 1572868
  158.2 6.4 %copy-start.11 = (bf16[4,4,64,256]{3,2,1,0:T(8,128)(2,1)S(1)}, bf16[4,4,64,256]{3,2,1,0:T(8,128)(2,1)}, u32[]{:S(2)}) copy-start(bf16[4,4,64,256]{3,2,1,0:T(8,128)(2,1)} %copy-done.10) | copy-start | bytes 1572868
  159.2 10.8 %all-to-all-start.6 = ((bf16[128,8,256]{2,1,0:T(8,128)(2,1)}), bf16[128,8,256]{2,1,0:T(8,128)(2,1)}, u32[]{:S(2)}, u32[]{:S(2)}) async-start(bf16[128,8,256]{2,1,0:T(8,128)(2,1)} %copy.398), calls=%async_computation.6 | async-start | bytes 1048576 | tf_op jit(solution)/shard_map/all_to_all | solution.py:226
  164.9 10.8 %copy-start.6 = (bf16[128,8,256]{2,0,1:T(8,128)(2,1)S(1)}, bf16[128,8,256]{2,0,1:T(8,128)(2,1)}, u32[]{:S(2)}) copy-start(bf16[128,8,256]{2,0,1:T(8,128)(2,1)} %copy-done.4) | copy-start | bytes 1572868
  169.2 8.9 %copy-start.18 = (bf16[128,8,256]{2,0,1:T(8,128)(2,1)S(1)}, bf16[128,8,256]{2,0,1:T(8,128)(2,1)}, u32[]{:S(2)}) copy-start(bf16[128,8,256]{2,0,1:T(8,128)(2,1)} %copy-done.17) | copy-start | bytes 1572868
  172.0 18.8 %all-to-all-start.7 = ((bf16[32,32,256]{2,1,0:T(8,128)(2,1)}), bf16[32,32,256]{2,1,0:T(8,128)(2,1)S(1)}, u32[]{:S(2)}, u32[]{:S(2)}) async-start(bf16[32,32,256]{2,1,0:T(8,128)(2,1)} %bitcast.254), calls=%async_computation.7 | async-start | bytes 1048576 | tf_op jit(solution)/shard_map/all_to_all | solution.py:225
  175.5 200.5 %all-reduce.4.cloned.1.call-start = ((), (), s32[]{:S(2)}) async-start(), calls=%async_computation.9 | async-start | bytes 8388608 | tf_op jit(solution)/shard_map/psum | solution.py:237
  197.7 8.0 %copy-start.30 = (bf16[4,256,256]{1,2,0:T(8,128)(2,1)S(1)}, bf16[4,256,256]{1,2,0:T(8,128)(2,1)}, u32[]{:S(2)}) copy-start(bf16[4,256,256]{1,2,0:T(8,128)(2,1)} %copy-done.29) | copy-start | bytes 1572868
  213.7 5.5 %copy-start.19 = (bf16[32,8,4,256]{3,1,2,0:T(8,128)(2,1)S(1)}, bf16[32,8,4,256]{3,1,2,0:T(8,128)(2,1)}, u32[]{:S(2)}) copy-start(bf16[32,8,4,256]{3,1,2,0:T(8,128)(2,1)} %copy.436) | copy-start | bytes 1572868
  213.7 6.5 %copy-start.16 = (bf16[4,256,256]{2,1,0:T(8,128)(2,1)S(1)}, bf16[4,256,256]{2,1,0:T(8,128)(2,1)}, u32[]{:S(2)}) copy-start(bf16[4,256,256]{2,1,0:T(8,128)(2,1)} %copy-done.15) | copy-start | bytes 1572868
  225.5 5.6 %copy-start.42 = (f32[256]{0:T(256)S(1)}, f32[256]{0:T(256)}, u32[]{:S(2)}) copy-start(f32[256]{0:T(256)} %get-tuple-element.73) | copy-start | bytes 3076
  225.5 5.6 %copy-start.43 = (f32[256]{0:T(256)S(1)}, f32[256]{0:T(256)}, u32[]{:S(2)}) copy-start(f32[256]{0:T(256)} %get-tuple-element.84) | copy-start | bytes 3076
  227.6 44.8 %all-to-all-start.8 = ((bf16[4,256,256]{2,0,1:T(4,128)(2,1)}), bf16[4,256,256]{2,0,1:T(4,128)(2,1)S(1)}, u32[]{:S(2)}, u32[]{:S(2)}) async-start(bf16[4,256,256]{2,0,1:T(4,128)(2,1)} %copy.408), calls=%async_computation.8 | async-start | bytes 1048576 | tf_op jit(solution)/shard_map/all_to_all | solution.py:235
  375.9 6.0 %copy-start.38 = (f32[256,256]{1,0:T(8,128)S(1)}, f32[256,256]{1,0:T(8,128)}, u32[]{:S(2)}) copy-start(f32[256,256]{1,0:T(8,128)} %get-tuple-element.143) | copy-start | bytes 786436
  375.9 6.7 %copy-start.24 = (f32[256,1024]{1,0:T(8,128)S(1)}, f32[256,1024]{1,0:T(8,128)}, u32[]{:S(2)}) copy-start(f32[256,1024]{1,0:T(8,128)} %get-tuple-element.145) | copy-start | bytes 3145732
  375.9 7.7 %copy-start.23 = (f32[1024,256]{1,0:T(8,128)S(1)}, f32[1024,256]{1,0:T(8,128)}, u32[]{:S(2)}) copy-start(f32[1024,256]{1,0:T(8,128)} %get-tuple-element.146) | copy-start | bytes 3145732
  378.1 6.4 %copy-start.1 = (bf16[256,1024]{1,0:T(8,128)(2,1)S(1)}, bf16[256,1024]{1,0:T(8,128)(2,1)}, u32[]{:S(2)}) copy-start(bf16[256,1024]{1,0:T(8,128)(2,1)} %param.22) | copy-start | bytes 1572868
  (23 other events, 54.8 us)
Sparse Core Ops, SparseCore 0:
  223.0 152.8 all-reduce.3
